TPU v7x, 128 devices: a whole 4x4x4 slice. The times are simulated.
128 devices in a mesh: space: 8 (over x, core), win: 16 (over z, y).
Axes of the slice: x: 4, y: 4, z: 4, core: 2. Of those that a mesh axis runs over, the one named last changes fastest.
Arguments:
- snapshots: bfloat16 [128, 24576, 256], P('win', 'space'), as said below
- modes: bfloat16 [128, 24576, 256], P('win', 'space'), may hold values from -0.5 to 0.5
- amp_re: float32 [128, 128], P('win'), may hold values from -5 to 5
- amp_im: float32 [128, 128], P('win'), may hold values from -5 to 5
- growth: float32 [128, 128], P('win'), may hold values from -0.01171875 to 0.001953125
- freq: float32 [128, 128], P('win'), may hold values from -3.140625 to 3.140625
- mode_count: int32 [128], P('win'), may hold values from 8 to 128
- slot_window: int32 [128], P('win'), may hold values from 0 to 127, as said below
Outputs:
- gram: float32 [128, 256, 256], P('win')
Inputs may be any that keep to these rules, and one draw needn't show every extreme that they name: slot_window is a permutation of the 128 windows; slot j holds a window of the same position in its block, slot_window[j] % 8 == j % 8; the 8 slots of one block hold windows of 8 different blocks. Each point's snapshots share one scale.
All inputs are finite; a program needn't handle non-finite values.
Results may differ from a plain program's by a relative error of at most 0.0026.
Values may be sent and summed in bfloat16 or wider, within the bound.
A program may use at most 192 MiB of HBM per device.

v0:
```python
import jax
import jax.numpy as jnp
from jax import lax
from jax.sharding import PartitionSpec as P

K = 128
S = 256
WIN_DEV = 8


def coefficients(amp_re, amp_im, growth, freq, mode_count):
    steps = jnp.arange(S).astype(jnp.float32)
    live = (jnp.arange(K, dtype=jnp.int32)[None, :] < mode_count[:, None]).astype(jnp.float32)
    decay = jnp.exp(growth[:, :, None] * steps) * live[:, :, None]
    angle = freq[:, :, None] * steps
    cosine = jnp.cos(angle)
    sine = jnp.sin(angle)
    real_part = (amp_re[:, :, None] * cosine - amp_im[:, :, None] * sine) * decay
    imag_part = (amp_re[:, :, None] * sine + amp_im[:, :, None] * cosine) * decay
    stacked = jnp.stack([real_part, -imag_part], axis=2)
    return stacked.reshape(amp_re.shape[0], 2 * K, S).astype(jnp.bfloat16)


def batch_grams(slabs, vectors, coef):
    recon = jnp.einsum("wpk,wks->wps", vectors, coef, preferred_element_type=jnp.float32)
    resid = (slabs.astype(jnp.float32) - recon).astype(jnp.bfloat16)
    return jnp.einsum("wps,wpt->wst", resid, resid, preferred_element_type=jnp.float32)


def on_device(snapshots, modes, amp_re, amp_im, growth, freq, mode_count, slot_window):
    nblocks = lax.axis_size("win")
    points_all = snapshots.shape[1] * lax.axis_size("space")
    coef = coefficients(amp_re, amp_im, growth, freq, mode_count)
    dest = slot_window // WIN_DEV
    place = slot_window % WIN_DEV
    vec_buf = jnp.zeros((nblocks,) + modes.shape[1:], jnp.bfloat16).at[dest].set(modes)
    coef_buf = jnp.zeros((nblocks, 2 * K, S), jnp.bfloat16).at[dest].set(coef)
    mark_buf = (
        jnp.zeros((nblocks, 128), jnp.bfloat16)
        .at[dest, place]
        .set(jnp.ones((WIN_DEV,), jnp.bfloat16))
    )
    got_vec, got_coef, got_mark = (
        lax.all_to_all(vec_buf, "win", split_axis=0, concat_axis=0, tiled=True),
        lax.all_to_all(coef_buf, "win", split_axis=0, concat_axis=0, tiled=True),
        lax.all_to_all(mark_buf, "win", split_axis=0, concat_axis=0, tiled=True),
    )
    marks = got_mark[:, :WIN_DEV].astype(jnp.int32)
    source = jnp.sum(jnp.arange(nblocks, dtype=jnp.int32)[:, None] * marks, axis=0)
    partial_value = batch_grams(snapshots, got_vec[source], got_coef[source])
    total = lax.psum(partial_value, "space")
    return total / points_all


def solution(mesh):
    return jax.shard_map(
        on_device,
        mesh=mesh,
        in_specs=(
            P("win", "space", None),
            P("win", "space", None),
            P("win", None),
            P("win", None),
            P("win", None),
            P("win", None),
            P("win"),
            P("win"),
        ),
        out_specs=P("win", None, None),
        check_vma=False,
    )
```

profile of v0, /device:TPU:0, one launch (start us, length us, event | category | flops | bytes accessed | tf_op | source)
XLA Modules:
  0.0 555.7 jit_solution(11417734754348130964)
XLA Ops:
  6.5 0.7 fusion.18
  7.2 0.9 scatter_fusion.1
  8.1 0.6 copy.20
  8.7 8.2 %all-to-all-start.1 = ((bf16[16,1,128]{2,1,0:T(2,128)(2,1)}), bf16[16,1,128]{2,1,0:T(2,128)(2,1)S(1)}, u32[]{:S(2)}, u32[]{:S(2)}) async-start(bf16[16,1,128]{2,1,0:T(2,128)(2,1)} %copy.20), calls=%async_computation.1 | async-start | bytes 16384 | tf_op jit(solution)/shard_map/all_to_all | solution.py:46
  16.9 0.7 fusion.14
  17.6 5.3 fusion.9
  22.9 0.1 pad_maximum_fusion
  23.1 0.6 copy.21
  23.6 0.2 copy.22
  23.9 1.5 broadcast_in_dim.14
  25.4 2.8 scatter_fusion.2
  28.2 0.0 all-to-all-done.1
  28.2 7.2 %all-to-all-start.2 = ((bf16[16,256,256]{2,1,0:T(8,128)(2,1)}), bf16[16,256,256]{2,1,0:T(8,128)(2,1)S(1)}, u32[]{:S(2)}, u32[]{:S(2)}) async-start(bf16[16,256,256]{2,1,0:T(8,128)(2,1)} %scatter_fusion.2), calls=%async_computation.2 | async-start | bytes 4194304 | tf_op jit(solution)/shard_map/all_to_all | solution.py:45
  35.5 8.3 %broadcast_in_dim.10 = bf16[16,3072,256]{2,1,0:T(8,128)(2,1)} broadcast(bf16[]{:T(256)} %constant.32.clone.1), dimensions={} | broadcast | bytes 25165826 | tf_op jit(solution)/shard_map/broadcast_in_dim | solution.py:36
  43.8 25.7 %scatter_fusion = bf16[16,3072,256]{2,1,0:T(8,128)(2,1)} fusion(bf16[16,3072,256]{2,1,0:T(8,128)(2,1)} %broadcast_in_dim.10, s32[8]{0:T(128)S(1)} %get-tuple-element.6, bf16[8,3072,256]{2,1,0:T(8,128)(2,1)} %param.9), kind=kCustom, calls=%fused_computation.2 | custom fusion | bytes 37748768 | tf_op jit(solution)/shard_map/scatter | solution.py:36
  69.5 0.0 all-to-all-done.2
  69.5 7.4 %all-to-all-start = ((bf16[16,3072,256]{2,1,0:T(8,128)(2,1)}), bf16[16,3072,256]{2,1,0:T(8,128)(2,1)}, u32[]{:S(2)}, u32[]{:S(2)}) async-start(bf16[16,3072,256]{2,1,0:T(8,128)(2,1)} %scatter_fusion), calls=%async_computation | async-start | bytes 50331648 | tf_op jit(solution)/shard_map/all_to_all | solution.py:44
  76.9 0.0 all-reduce.2.cloned.1.call-start
  77.0 0.6 gather_fusion.1
  77.6 369.2 %all-to-all-done = bf16[16,3072,256]{2,1,0:T(8,128)(2,1)} async-done(((bf16[16,3072,256]{2,1,0:T(8,128)(2,1)}), bf16[16,3072,256]{2,1,0:T(8,128)(2,1)}, u32[]{:S(2)}, u32[]{:S(2)}) %all-to-all-start) | async-done | bytes 25165856 | tf_op jit(solution)/shard_map/all_to_all | solution.py:44
  446.8 14.6 %gather_fusion = bf16[8,3072,256]{2,1,0:T(8,128)(2,1)} fusion(bf16[16,3072,256]{2,1,0:T(8,128)(2,1)} %all-to-all-done, s32[1024]{0:T(1024)S(1)} %pad_clamp_fusion), kind=kCustom, calls=%fused_computation | custom fusion | bytes 25165856 | tf_op jit(solution)/shard_map/gather | solution.py:50
  461.4 19.9 %fusion = f32[8,256,256]{2,1,0:T(8,128)} fusion(bf16[8,3072,256]{2,1,0:T(8,128)(2,1)} %param.8, bf16[8,3072,256]{2,1,0:T(8,128)(2,1)} %gather_fusion, bf16[8,256,256]{2,1,0:T(8,128)(2,1)S(1)} %gather_fusion.1), kind=kOutput, calls=%fused_computation.6 | convolution fusion | flops 6461325312 | bytes 28311552 | tf_op jit(solution)/shard_map/wps,wpt->wst/dot_general | solution.py:27
  481.3 0.0 all-reduce.2.cloned.1.call-update
  481.4 64.4 %all-reduce.2.cloned.1.call-done = f32[8,256,256]{2,1,0:T(8,128)} async-done(((f32[8,256,256]{2,1,0:T(8,128)}), f32[8,256,256]{2,1,0:T(8,128)}) %all-reduce.2.cloned.1.call-update) | async-done | bytes 2097168 | tf_op jit(solution)/shard_map/psum | solution.py:51
  545.8 3.1 broadcast_multiply_fusion
  (7 shorter events, 0.1 us)
Async XLA Ops:
  8.7 19.5 %all-to-all-start.1 = ((bf16[16,1,128]{2,1,0:T(2,128)(2,1)}), bf16[16,1,128]{2,1,0:T(2,128)(2,1)S(1)}, u32[]{:S(2)}, u32[]{:S(2)}) async-start(bf16[16,1,128]{2,1,0:T(2,128)(2,1)} %copy.20), calls=%async_computation.1 | async-start | bytes 16384 | tf_op jit(solution)/shard_map/all_to_all | solution.py:46
  28.2 41.2 %all-to-all-start.2 = ((bf16[16,256,256]{2,1,0:T(8,128)(2,1)}), bf16[16,256,256]{2,1,0:T(8,128)(2,1)S(1)}, u32[]{:S(2)}, u32[]{:S(2)}) async-start(bf16[16,256,256]{2,1,0:T(8,128)(2,1)} %scatter_fusion.2), calls=%async_computation.2 | async-start | bytes 4194304 | tf_op jit(solution)/shard_map/all_to_all | solution.py:45
  69.5 377.3 %all-to-all-start = ((bf16[16,3072,256]{2,1,0:T(8,128)(2,1)}), bf16[16,3072,256]{2,1,0:T(8,128)(2,1)}, u32[]{:S(2)}, u32[]{:S(2)}) async-start(bf16[16,3072,256]{2,1,0:T(8,128)(2,1)} %scatter_fusion), calls=%async_computation | async-start | bytes 50331648 | tf_op jit(solution)/shard_map/all_to_all | solution.py:44
  76.9 468.9 %all-reduce.2.cloned.1.call-start = ((), (), s32[]{:S(2)}) async-start(), calls=%async_computation.3 | async-start | bytes 4194304 | tf_op jit(solution)/shard_map/psum | solution.py:51
Sparse Core Ops, SparseCore 0:
  481.5 64.2 all-reduce.1
where the time goes:
time: 556 us
  waiting for transfers between devices  434 us (78%)
  local copies, waits for them, and re-layouts  55.9 us (10%)
  starting transfers between devices  22.8 us (4%)
  matrix products  19.9 us (4%)
  between operations  13.5 us (2%)
  other arithmetic  9.96 us (2%)
    all_to_all x1, waiting for transfers between devices, on_device(): lax.all_to_all(vec_buf, 'win', split_axis=0, concat_axis=0, tiled=True)  369 us
    psum x1, waiting for transfers between devices, on_device(): total = lax.psum(partial_value, 'space')  64.4 us
    scatter x1, local copies, waits for them, and re-layouts, on_device(): jnp.zeros((nblocks,) + modes.shape[1:], jnp.bfloat16).at[dest].set(modes)  25.7 us
    dot_general x1, matrix products, batch_grams(): jnp.einsum('wps,wpt->wst', resid, resid, preferred_element_type=jnp.float32)  19.9 us
    gather x2, local copies, waits for them, and re-layouts, on_device(): partial_value = batch_grams(snapshots, got_vec[source], got_coef[source])  15.2 us
  transfers between devices with their start and end apart: 4, of which 2 were waited for; matrix products, arithmetic and copies ran while one was open for 8% of the time, Pallas kernels for 0%

commit v1 on v0

--- a/solution.py
+++ b/solution.py
@@ -48,7 +48,13 @@
     marks = got_mark[:, :WIN_DEV].astype(jnp.int32)
     source = jnp.sum(jnp.arange(nblocks, dtype=jnp.int32)[:, None] * marks, axis=0)
     partial_value = batch_grams(snapshots, got_vec[source], got_coef[source])
-    total = lax.psum(partial_value, "space")
+    p_count = lax.axis_size("space")
+    total, x_now = (partial_value, 0)
+    while 1 << x_now < p_count:
+        found_now = tuple(((num, num ^ 1 << x_now) for num in range(p_count)))
+        next_value = lax.ppermute(total, "space", found_now)
+        total = total + next_value
+        x_now = x_now + 1
     return total / points_all
 
 

time: 556 us -> 582 us (1.047)
  waiting for transfers between devices: 434 us -> 465 us
  between operations: 13.5 us -> 0.13 us
    ppermute x0 -> x3, waiting for transfers between devices: none -> 95.6 us  [on_device(): next_value = lax.ppermute(total, 'space', found_now)]
    psum x1 -> x0, waiting for transfers between devices: 64.4 us -> none  [on_device(): total = lax.psum(partial_value, 'space')]
  transfers between devices with their start and end apart: 4 -> 6, of which waited for: 2 -> 4; matrix products, arithmetic and copies ran while one was open for 8% -> 8% of each run, Pallas kernels for 0% -> 0%
where the time goes in v1:
time: 582 us
  waiting for transfers between devices  465 us (80%)
  local copies, waits for them, and re-layouts  55.9 us (10%)
  starting transfers between devices  27.5 us (5%)
  matrix products  24.3 us (4%)
  other arithmetic  9.2 us (2%)
    all_to_all x1, waiting for transfers between devices, on_device(): lax.all_to_all(vec_buf, 'win', split_axis=0, concat_axis=0, tiled=True)  369 us
    ppermute x3, waiting for transfers between devices, on_device(): next_value = lax.ppermute(total, 'space', found_now)  95.6 us
    scatter x1, local copies, waits for them, and re-layouts, on_device(): jnp.zeros((nblocks,) + modes.shape[1:], jnp.bfloat16).at[dest].set(modes)  25.7 us
    dot_general x1, matrix products, batch_grams(): jnp.einsum('wps,wpt->wst', resid, resid, preferred_element_type=jnp.float32)  24.3 us
    gather x2, local copies, waits for them, and re-layouts, on_device(): partial_value = batch_grams(snapshots, got_vec[source], got_coef[source])  15.2 us
  transfers between devices with their start and end apart: 6, of which 4 were waited for; matrix products, arithmetic and copies ran while one was open for 8% of the time, Pallas kernels for 0%

profile of v1, /device:TPU:0, one launch (start us, length us, event | category | flops | bytes accessed | tf_op | source)
XLA Modules:
  0.0 582.0 jit_solution(14621070001733090956)
XLA Ops:
  0.0 0.7 fusion.18
  0.7 0.9 scatter_fusion.1
  1.6 0.6 copy.20
  2.2 8.2 %all-to-all-start.1 = ((bf16[16,1,128]{2,1,0:T(2,128)(2,1)}), bf16[16,1,128]{2,1,0:T(2,128)(2,1)S(1)}, u32[]{:S(2)}, u32[]{:S(2)}) async-start(bf16[16,1,128]{2,1,0:T(2,128)(2,1)} %copy.20), calls=%async_computation.1 | async-start | bytes 16384 | tf_op jit(solution)/shard_map/all_to_all | solution.py:46
  10.3 0.7 fusion.14
  11.1 5.3 fusion.9
  16.4 0.1 pad_maximum_fusion
  16.5 0.6 copy.21
  17.1 0.2 copy.22
  17.3 1.5 broadcast_in_dim.14
  18.9 2.8 scatter_fusion.2
  21.7 0.0 all-to-all-done.1
  21.7 7.2 %all-to-all-start.2 = ((bf16[16,256,256]{2,1,0:T(8,128)(2,1)}), bf16[16,256,256]{2,1,0:T(8,128)(2,1)S(1)}, u32[]{:S(2)}, u32[]{:S(2)}) async-start(bf16[16,256,256]{2,1,0:T(8,128)(2,1)} %scatter_fusion.2), calls=%async_computation.2 | async-start | bytes 4194304 | tf_op jit(solution)/shard_map/all_to_all | solution.py:45
  28.9 8.4 %broadcast_in_dim.10 = bf16[16,3072,256]{2,1,0:T(8,128)(2,1)} broadcast(bf16[]{:T(256)} %constant.32.clone.1), dimensions={} | broadcast | bytes 25165826 | tf_op jit(solution)/shard_map/broadcast_in_dim | solution.py:36
  37.3 25.7 %scatter_fusion = bf16[16,3072,256]{2,1,0:T(8,128)(2,1)} fusion(bf16[16,3072,256]{2,1,0:T(8,128)(2,1)} %broadcast_in_dim.10, s32[8]{0:T(128)S(1)} %get-tuple-element.6, bf16[8,3072,256]{2,1,0:T(8,128)(2,1)} %param.9), kind=kCustom, calls=%fused_computation.2 | custom fusion | bytes 37748768 | tf_op jit(solution)/shard_map/scatter | solution.py:36
  62.9 0.0 all-to-all-done.2
  62.9 7.4 %all-to-all-start = ((bf16[16,3072,256]{2,1,0:T(8,128)(2,1)}), bf16[16,3072,256]{2,1,0:T(8,128)(2,1)}, u32[]{:S(2)}, u32[]{:S(2)}) async-start(bf16[16,3072,256]{2,1,0:T(8,128)(2,1)} %scatter_fusion), calls=%async_computation | async-start | bytes 50331648 | tf_op jit(solution)/shard_map/all_to_all | solution.py:44
  70.4 0.6 gather_fusion.1
  71.0 369.3 %all-to-all-done = bf16[16,3072,256]{2,1,0:T(8,128)(2,1)} async-done(((bf16[16,3072,256]{2,1,0:T(8,128)(2,1)}), bf16[16,3072,256]{2,1,0:T(8,128)(2,1)}, u32[]{:S(2)}, u32[]{:S(2)}) %all-to-all-start) | async-done | bytes 25165856 | tf_op jit(solution)/shard_map/all_to_all | solution.py:44
  440.3 14.6 %gather_fusion = bf16[8,3072,256]{2,1,0:T(8,128)(2,1)} fusion(bf16[16,3072,256]{2,1,0:T(8,128)(2,1)} %all-to-all-done, s32[1024]{0:T(1024)S(1)} %pad_clamp_fusion), kind=kCustom, calls=%fused_computation | custom fusion | bytes 25165856 | tf_op jit(solution)/shard_map/gather | solution.py:50
  454.9 24.3 %fusion = f32[8,256,256]{2,1,0:T(8,128)S(1)} fusion(bf16[8,3072,256]{2,1,0:T(8,128)(2,1)} %param.8, bf16[8,3072,256]{2,1,0:T(8,128)(2,1)} %gather_fusion, bf16[8,256,256]{2,1,0:T(8,128)(2,1)S(1)} %gather_fusion.1), kind=kOutput, calls=%fused_computation.6 | convolution fusion | flops 6461325312 | bytes 28311552 | tf_op jit(solution)/shard_map/wps,wpt->wst/dot_general | solution.py:27
  479.2 0.1 collective-permute-start
  479.3 4.1 collective-permute-done
  483.5 0.4 add.50
  483.9 1.6 collective-permute-start.1
  485.4 46.2 %collective-permute-done.1 = f32[8,256,256]{2,1,0:T(8,128)S(1)} collective-permute-done((f32[8,256,256]{2,1,0:T(8,128)S(1)}, f32[8,256,256]{2,1,0:T(8,128)S(1)}, u32[]{:S(2)}, u32[]{:S(2)}) %collective-permute-start.1) | collective-permute-done | bytes 2097184 | tf_op jit(solution)/shard_map/ppermute | solution.py:55
  531.6 0.3 add.51
  531.9 3.1 collective-permute-start.2
  535.0 45.3 %collective-permute-done.2 = f32[8,256,256]{2,1,0:T(8,128)S(1)} collective-permute-done((f32[8,256,256]{2,1,0:T(8,128)S(1)}, f32[8,256,256]{2,1,0:T(8,128)S(1)}, u32[]{:S(2)}, u32[]{:S(2)}) %collective-permute-start.2) | collective-permute-done | bytes 2097184 | tf_op jit(solution)/shard_map/ppermute | solution.py:55
  580.3 1.7 add_multiply_fusion
  (7 shorter events, 0.1 us)
Async XLA Ops:
  2.2 19.5 %all-to-all-start.1 = ((bf16[16,1,128]{2,1,0:T(2,128)(2,1)}), bf16[16,1,128]{2,1,0:T(2,128)(2,1)S(1)}, u32[]{:S(2)}, u32[]{:S(2)}) async-start(bf16[16,1,128]{2,1,0:T(2,128)(2,1)} %copy.20), calls=%async_computation.1 | async-start | bytes 16384 | tf_op jit(solution)/shard_map/all_to_all | solution.py:46
  21.7 41.2 %all-to-all-start.2 = ((bf16[16,256,256]{2,1,0:T(8,128)(2,1)}), bf16[16,256,256]{2,1,0:T(8,128)(2,1)S(1)}, u32[]{:S(2)}, u32[]{:S(2)}) async-start(bf16[16,256,256]{2,1,0:T(8,128)(2,1)} %scatter_fusion.2), calls=%async_computation.2 | async-start | bytes 4194304 | tf_op jit(solution)/shard_map/all_to_all | solution.py:45
  62.9 377.3 %all-to-all-start = ((bf16[16,3072,256]{2,1,0:T(8,128)(2,1)}), bf16[16,3072,256]{2,1,0:T(8,128)(2,1)}, u32[]{:S(2)}, u32[]{:S(2)}) async-start(bf16[16,3072,256]{2,1,0:T(8,128)(2,1)} %scatter_fusion), calls=%async_computation | async-start | bytes 50331648 | tf_op jit(solution)/shard_map/all_to_all | solution.py:44
  479.2 4.2 collective-permute-start
  483.9 47.8 %collective-permute-start.1 = (f32[8,256,256]{2,1,0:T(8,128)S(1)}, f32[8,256,256]{2,1,0:T(8,128)S(1)}, u32[]{:S(2)}, u32[]{:S(2)}) collective-permute-start(f32[8,256,256]{2,1,0:T(8,128)S(1)} %add.50), channel_id=1, source_target_pairs={{0,32},{16,48},{32,0},{48,16},{64,96},{80,112},{96,64},{112,80},{1... | collective-permute-start | bytes 6291464 | tf_op jit(solution)/shard_map/ppermute | solution.py:55
  531.9 48.4 %collective-permute-start.2 = (f32[8,256,256]{2,1,0:T(8,128)S(1)}, f32[8,256,256]{2,1,0:T(8,128)S(1)}, u32[]{:S(2)}, u32[]{:S(2)}) collective-permute-start(f32[8,256,256]{2,1,0:T(8,128)S(1)} %add.51), channel_id=1, source_target_pairs={{0,64},{16,80},{32,96},{48,112},{64,0},{80,16},{96,32},{112,48},{1... | collective-permute-start | bytes 6291464 | tf_op jit(solution)/shard_map/ppermute | solution.py:55
